TPU v7x, 32 devices: a whole 2x2x4 slice. The times are simulated.
32 devices in a mesh: grp: 2 (over y), seq: 8 (over z, x), mdl: 2 (over core).
Axes of the slice: x: 2, y: 2, z: 4, core: 2. Of those that a mesh axis runs over, the one named last changes fastest.
Arguments:
- signal: bfloat16 [2048, 2048], P(('grp', 'seq'), 'mdl'), parts along dimension 0, may hold values from -6 to 6
- gate_first: bfloat16 [2048, 2048], P(('grp', 'seq'), 'mdl'), parts along dimension 0, may hold values from -6 to 6
- gate_second: bfloat16 [2048, 2048], P(('grp', 'seq'), 'mdl'), parts along dimension 0, may hold values from -6 to 6
- spectrum_first: bfloat16 [2, 16, 128, 2048], P(None, 'seq', None, 'mdl'), may hold values from -8 to 8
- spectrum_second: bfloat16 [2, 16, 128, 2048], P(None, 'seq', None, 'mdl'), may hold values from -8 to 8
- skip_first: float32 [2048], P('mdl'), may hold values from 0.5 to 1.5
- skip_second: float32 [2048], P('mdl'), may hold values from 0.5 to 1.5
- out_weight: bfloat16 [2048, 2048], P('seq', 'mdl'), may hold values from -0.125 to 0.125
Outputs:
- block_out: bfloat16 [2048, 2048], P(('grp', 'seq'), 'mdl'), parts along dimension 0
There are 2 independent parts, one for each index of `grp`. A program takes and returns all parts, laid end to end along the dimension named above; an argument that names none is the same for every part. Nothing has to cross between parts.
All inputs are finite; a program needn't handle non-finite values.
Results may differ from a plain program's by a relative error of at most 0.0057.
Values may be sent and summed in bfloat16 or wider, within the bound.
A program may use at most 64 MiB of HBM per device.

v0:
```python
import math
import jax
import jax.numpy as jnp
from jax import lax
from jax.sharding import PartitionSpec as P


def angle_grid(first, second, modulus):
    product = first[:, None] * second[None, :] % modulus
    angles = product.astype(jnp.float32) * (2.0 * math.pi / modulus)
    return (jnp.cos(angles), jnp.sin(angles))


def mixing(form, left, right):
    return jnp.einsum(form, left, right, precision=lax.Precision.HIGHEST)


def complex_mix(form, real_table, imag_table, values_re, values_im):
    first_term = mixing(form, real_table, values_re + values_im)
    second_term = mixing(form, real_table + imag_table, values_im)
    third_term = mixing(form, imag_table - real_table, values_re)
    return (first_term - second_term, first_term + third_term)


def channel_filter(field, spectrum):
    coarse = spectrum.shape[1]
    span = spectrum.shape[2]
    count = coarse // 2
    cols = field.shape[1]
    length = coarse * span
    pencil = field.reshape(count, span, cols)
    coarse_ids = jnp.arange(coarse, dtype=jnp.int32)
    cos_a, sin_a = angle_grid(coarse_ids, jnp.arange(count, dtype=jnp.int32), coarse)
    part_re = mixing("ka,amc->kmc", cos_a, pencil)
    part_im = -mixing("ka,amc->kmc", sin_a, pencil)
    fine_ids = jnp.arange(span, dtype=jnp.int32)
    cos_t, sin_t = angle_grid(coarse_ids, fine_ids, length)
    cos_t = cos_t[:, :, None]
    sin_t = sin_t[:, :, None]
    turned_re = part_re * cos_t + part_im * sin_t
    turned_im = part_im * cos_t - part_re * sin_t
    cos_s, sin_s = angle_grid(fine_ids, fine_ids, span)
    full_re, full_im = complex_mix("qm,kmc->kqc", cos_s, -sin_s, turned_re, turned_im)
    filt_re = spectrum[0].astype(jnp.float32)
    filt_im = spectrum[1].astype(jnp.float32)
    prod_re = filt_re * full_re - filt_im * full_im
    prod_im = filt_re * full_im + filt_im * full_re
    inner_re, inner_im = complex_mix("mq,kqc->kmc", cos_s, sin_s, prod_re, prod_im)
    back_re = inner_re * cos_t - inner_im * sin_t
    back_im = inner_im * cos_t + inner_re * sin_t
    result = mixing("ka,kmc->amc", cos_a, back_re) - mixing("ka,kmc->amc", sin_a, back_im)
    return (result / length).reshape(count * span, cols)


def shards(
    signal,
    gate_first,
    gate_second,
    spectrum_first,
    spectrum_second,
    skip_first,
    skip_second,
    out_weight,
):
    seq_index = lax.axis_index("seq")
    width = signal.shape[1]
    parts_seq = lax.axis_size("seq")
    cols = width // parts_seq
    col_sig, col_first, col_second = (
        lax.all_to_all(signal, "seq", split_axis=1, concat_axis=0, tiled=True),
        lax.all_to_all(gate_first, "seq", split_axis=1, concat_axis=0, tiled=True),
        lax.all_to_all(gate_second, "seq", split_axis=1, concat_axis=0, tiled=True),
    )
    spec_one, spec_two = (
        lax.all_to_all(spectrum_first, "seq", split_axis=3, concat_axis=1, tiled=True),
        lax.all_to_all(spectrum_second, "seq", split_axis=3, concat_axis=1, tiled=True),
    )
    skip_one = lax.dynamic_slice_in_dim(skip_first, seq_index * cols, cols, 0)
    skip_two = lax.dynamic_slice_in_dim(skip_second, seq_index * cols, cols, 0)
    values = col_sig.astype(jnp.float32)
    first_conv = channel_filter(values, spec_one) + skip_one * values
    first_out = (col_first.astype(jnp.float32) * first_conv).astype(jnp.bfloat16)
    first_vals = first_out.astype(jnp.float32)
    second_conv = channel_filter(first_vals, spec_two) + skip_two * first_vals
    mixed_cols = (col_second.astype(jnp.float32) * second_conv).astype(jnp.bfloat16)
    mixed = lax.all_to_all(mixed_cols, "seq", split_axis=0, concat_axis=1, tiled=True)
    features = lax.all_gather(mixed, "mdl", axis=1, tiled=True)
    total = jnp.dot(
        features,
        lax.all_gather(out_weight, "seq", axis=0, tiled=True),
        preferred_element_type=jnp.float32,
    )
    return total.astype(jnp.bfloat16)


def solution(mesh):
    placed = (
        P(("grp", "seq"), "mdl"),
        P(("grp", "seq"), "mdl"),
        P(("grp", "seq"), "mdl"),
        P(None, "seq", None, "mdl"),
        P(None, "seq", None, "mdl"),
        P("mdl"),
        P("mdl"),
        P("seq", "mdl"),
    )
    return jax.shard_map(
        shards, mesh=mesh, in_specs=placed, out_specs=P(("grp", "seq"), "mdl"), check_vma=False
    )
```

profile of v0, /device:TPU:0, one launch (start us, length us, event | category | flops | bytes accessed | tf_op | source)
XLA Modules:
  0.0 189.6 jit_solution(12314016013267601482)
XLA Ops:
  6.5 1.2 copy.80
  7.8 0.9 copy.81
  8.6 7.4 %all-to-all-start.4 = ((bf16[128,8,128]{2,0,1:T(8,128)(2,1)}), bf16[128,8,128]{2,0,1:T(8,128)(2,1)S(1)}, u32[]{:S(2)}, u32[]{:S(2)}) async-start(bf16[128,8,128]{2,0,1:T(8,128)(2,1)} %copy.81), calls=%async_computation.4 | async-start | bytes 524288 | tf_op jit(solution)/shard_map/all_to_all | solution.py:70
  16.0 3.7 %copy.78 = bf16[2,2,128,1024]{2,1,0,3:T(2,128)(2,1)} copy(bf16[2,2,128,1024]{3,2,1,0:T(8,128)(2,1)} %param.11) | data formatting | bytes 2097152 | tf_op args[3]
  19.7 5.2 %all-to-all-done.4 = bf16[128,8,128]{2,0,1:T(8,128)(2,1)S(1)} async-done(((bf16[128,8,128]{2,0,1:T(8,128)(2,1)}), bf16[128,8,128]{2,0,1:T(8,128)(2,1)S(1)}, u32[]{:S(2)}, u32[]{:S(2)}) %all-to-all-start.4) | async-done | bytes 262176 | tf_op jit(solution)/shard_map/all_to_all | solution.py:70
  24.9 3.6 %all-to-all-start.3 = ((bf16[2,2,128,1024]{2,1,0,3:T(2,128)(2,1)}), bf16[2,2,128,1024]{2,1,0,3:T(2,128)(2,1)S(1)}, u32[]{:S(2)}, u32[]{:S(2)}) async-start(bf16[2,2,128,1024]{2,1,0,3:T(2,128)(2,1)} %copy.78), calls=%async_computation.3 | async-start | bytes 2097152 | tf_op jit(solution)/shard_map/all_to_all | solution.py:75
  28.5 0.0 all-gather.2.cloned.1.call-start
  28.6 0.7 all-gather.2.cloned.1.call-update
  29.2 0.1 fusion.83
  29.3 0.1 copy.83
  29.4 0.1 copy.84
  29.5 0.0 copy-done.2
  29.5 0.2 copy.75
  29.7 0.9 copy.76
  30.6 0.0 copy-done.1
  30.6 2.0 %copy.73 = bf16[2,2,128,1024]{2,1,0,3:T(2,128)(2,1)} copy(bf16[2,2,128,1024]{3,2,1,0:T(8,128)(2,1)S(1)} %copy-done.1) | data formatting | bytes 2097152 | tf_op args[4]
  32.6 1.3 dynamic_slice.6
  33.9 1.3 dynamic_slice.7
  35.3 0.0 copy-done.3
  35.3 0.2 copy.70
  35.5 0.9 copy.71
  36.3 0.7 convolution_negate_fusion.1
  37.0 2.6 %fusion.179 = (f32[16,128,128]{2,0,1:T(8,128)S(1)}, f32[16,128,128]{2,0,1:T(8,128)S(1)}, f32[16,128,128]{2,0,1:T(8,128)}) fusion(f32[16,128]{0,1:T(8,128)S(1)} %copy.84, f32[16,128,128]{2,0,1:T(8,128)S(1)} %convolution_negate_fusion.1, f32[16,128]{0,1:T(8,128)S(1)} %copy.83, bf16[128,8,128]{2,0,1:T(8,128)(2,1)S(1)} %all-to-all-done.4), kind=kOutput, calls=%fused_computation.205 | convolution fusion | flops 27002624 | bytes 4472832 | tf_op jit(solution)/shard_map/ka,amc->kmc/dot_general | solution.py:15
  39.6 29.2 %all-to-all-done.3 = bf16[2,2,128,1024]{2,1,0,3:T(2,128)(2,1)S(1)} async-done(((bf16[2,2,128,1024]{2,1,0,3:T(2,128)(2,1)}), bf16[2,2,128,1024]{2,1,0,3:T(2,128)(2,1)S(1)}, u32[]{:S(2)}, u32[]{:S(2)}) %all-to-all-start.3) | async-done | bytes 1048608 | tf_op jit(solution)/shard_map/all_to_all | solution.py:75
  68.8 4.4 %all-to-all-start.1 = ((bf16[2,2,128,1024]{2,1,0,3:T(2,128)(2,1)}), bf16[2,2,128,1024]{2,1,0,3:T(2,128)(2,1)}, u32[]{:S(2)}, u32[]{:S(2)}) async-start(bf16[2,2,128,1024]{2,1,0,3:T(2,128)(2,1)} %copy.73), calls=%async_computation.1 | async-start | bytes 2097152 | tf_op jit(solution)/shard_map/all_to_all | solution.py:76
  73.3 2.1 %fusion.22 = f32[16,128,128]{2,1,0:T(8,128)S(1)} fusion(f32[16,128,128]{2,0,1:T(8,128)S(1)} %get-tuple-element.8), kind=kOutput, calls=%fused_computation.43 | convolution fusion | flops 402882560 | bytes 2097152 | tf_op jit(solution)/shard_map/qm,kmc->kqc/dot_general | solution.py:15
  75.4 0.0 copy-start
  75.4 2.2 %fusion.3 = f32[16,128,128]{1,2,0:T(8,128)S(1)} fusion(f32[16,128,128]{2,1,0:T(8,128)S(1)} %fusion.22, f32[16,128,128]{2,0,1:T(8,128)S(1)} %get-tuple-element.9), kind=kOutput, calls=%fused_computation.12 | convolution fusion | flops 403177472 | bytes 3145728 | tf_op jit(solution)/shard_map/qm,kmc->kqc/dot_general | solution.py:15
  77.6 0.2 copy.128
  77.8 0.1 fusion.181
  77.9 0.0 copy-done
  77.9 2.4 %fusion.13 = (f32[16,128,128]{1,2,0:T(8,128)S(1)}, f32[16,128,128]{1,2,0:T(8,128)S(1)}) fusion(f32[16,128,128]{1,2,0:T(8,128)S(1)} %fusion.3, bf16[1,8,2,128,128]{3,4,2,1,0:T(8,128)(2,1)S(1)} %get-tuple-element.22, bf16[1,8,2,128,128]{3,4,2,1,0:T(8,128)(2,1)S(1)} %get-tuple-element.21, f32[16,128,128]{2,1,0:T(8,128)S(1)} %fusion.22, ...), kind=kOutput, calls=%fused_computation.34 | convolution fusion | flops 405274624 | bytes 6291456 | tf_op jit(solution)/shard_map/qm,kmc->kqc/dot_general | solution.py:15
  80.3 1.2 fusion.26
  81.6 1.2 convolution_add_fusion.2
  82.8 40.1 %all-to-all-done.1 = bf16[2,2,128,1024]{2,1,0,3:T(2,128)(2,1)} async-done(((bf16[2,2,128,1024]{2,1,0,3:T(2,128)(2,1)}), bf16[2,2,128,1024]{2,1,0,3:T(2,128)(2,1)}, u32[]{:S(2)}, u32[]{:S(2)}) %all-to-all-start.1) | async-done | bytes 1048608 | tf_op jit(solution)/shard_map/all_to_all | solution.py:76
  122.9 4.3 %all-to-all-start.2 = ((bf16[128,8,128]{2,0,1:T(8,128)(2,1)}), bf16[128,8,128]{2,0,1:T(8,128)(2,1)}, u32[]{:S(2)}, u32[]{:S(2)}) async-start(bf16[128,8,128]{2,0,1:T(8,128)(2,1)} %copy.76), calls=%async_computation.2 | async-start | bytes 524288 | tf_op jit(solution)/shard_map/all_to_all | solution.py:71
  127.2 2.8 %add_bitcast_fusion.1 = (f32[16,128,128]{1,2,0:T(8,128)}, f32[16,128,128]{1,2,0:T(8,128)}) fusion(f32[16,128,128]{2,1,0:T(8,128)S(1)} %convolution_add_fusion.2, f32[16,128]{1,0:T(8,128)S(1)} %get-tuple-element.23, f32[16,128]{1,0:T(8,128)S(1)} %get-tuple-element.24, f32[16,128,128]{2,1,0:T(8,128)S(1)} %fusion.26, f32[16,128,128]{1,2,0:T(8,128)S(1)} %get-tuple-element.13), kind=kOutput, calls=%fused_computation.53 | convolution fusion | flops 404733952 | bytes 5259264 | tf_op jit(solution)/shard_map/mq,kqc->kmc/dot_general | solution.py:15
  130.0 2.6 %copy.88 = f32[16,128,128]{2,0,1:T(8,128)} copy(f32[16,128,128]{1,2,0:T(8,128)} %get-tuple-element.18) | data formatting | bytes 2097152 | tf_op jit(solution)/shard_map/sub | solution.py:49
  132.6 1.7 copy.89
  134.3 1.5 copy.129
  135.8 1.9 fusion.80
  137.7 0.0 all-to-all-done.2
  137.7 5.7 %all-to-all-start = ((bf16[128,8,128]{2,0,1:T(8,128)(2,1)}), bf16[128,8,128]{2,0,1:T(8,128)(2,1)S(1)}, u32[]{:S(2)}, u32[]{:S(2)}) async-start(bf16[128,8,128]{2,0,1:T(8,128)(2,1)} %copy.71), calls=%async_computation | async-start | bytes 524288 | tf_op jit(solution)/shard_map/all_to_all | solution.py:72
  143.4 1.9 fusion.11
  145.2 0.7 convolution_negate_fusion
  145.9 0.1 fusion.180
  146.0 1.1 fusion.178
  147.1 2.1 %fusion.18 = f32[16,128,128]{2,1,0:T(8,128)S(1)} fusion(f32[16,128,128]{2,0,1:T(8,128)S(1)} %get-tuple-element.5), kind=kOutput, calls=%fused_computation.39 | convolution fusion | flops 402882560 | bytes 2097152 | tf_op jit(solution)/shard_map/qm,kmc->kqc/dot_general | solution.py:15
  149.2 2.2 %fusion.1 = f32[16,128,128]{1,2,0:T(8,128)S(1)} fusion(f32[16,128,128]{2,1,0:T(8,128)S(1)} %fusion.18, f32[16,128,128]{2,0,1:T(8,128)S(1)} %get-tuple-element.6), kind=kOutput, calls=%fused_computation.5 | convolution fusion | flops 403177472 | bytes 3145728 | tf_op jit(solution)/shard_map/qm,kmc->kqc/dot_general | solution.py:15
  151.4 2.4 %fusion.15 = (f32[16,128,128]{1,2,0:T(8,128)S(1)}, f32[16,128,128]{1,2,0:T(8,128)S(1)}) fusion(f32[16,128,128]{1,2,0:T(8,128)S(1)} %fusion.1, bf16[1,8,2,128,128]{3,4,2,1,0:T(8,128)(2,1)S(1)} %get-tuple-element.20, bf16[1,8,2,128,128]{3,4,2,1,0:T(8,128)(2,1)S(1)} %get-tuple-element.19, f32[16,128,128]{2,1,0:T(8,128)S(1)} %fusion.18, ...), kind=kOutput, calls=%fused_computation.36 | convolution fusion | flops 405274624 | bytes 6291456 | tf_op jit(solution)/shard_map/qm,kmc->kqc/dot_general | solution.py:15
  153.8 1.2 fusion.24
  155.1 1.3 convolution_add_fusion
  156.3 1.7 add_bitcast_fusion
  158.0 0.0 copy-start.4
  158.0 1.4 copy.93
  159.4 0.5 copy.94
  160.0 1.9 fusion.76
  161.8 0.0 all-to-all-done
  161.8 0.0 copy-done.4
  161.8 0.8 fusion.10
  162.7 14.0 %all_to_all.88 = bf16[8,128,128]{2,1,0:T(8,128)(2,1)S(1)} all-to-all(bf16[8,128,128]{2,1,0:T(8,128)(2,1)S(1)} %copy.95), channel_id=1, replica_groups=mesh['grp'=2,'seq'=8,'mdl'=2] {'seq'}, dimensions={0} | all-to-all | bytes 524288 | tf_op jit(solution)/shard_map/all_to_all | solution.py:86
  176.7 0.2 copy.96
  176.9 2.2 %all_gather.6 = bf16[128,2048]{0,1:T(8,128)(2,1)S(1)} all-gather(bf16[128,1024]{0,1:T(8,128)(2,1)S(1)} %bitcast.132), channel_id=1, replica_groups=mesh['grp'=2,'seq'=8,'mdl'=2] {'mdl'}, dimensions={1}, use_global_device_ids=true | all-gather | bytes 786432 | tf_op jit(solution)/shard_map/all_gather | solution.py:87
  179.1 3.6 %convolution_convert_fusion = bf16[128,1024]{1,0:T(8,128)(2,1)} fusion(bf16[128,2048]{0,1:T(8,128)(2,1)S(1)} %all_gather.6, bf16[2048,1024]{1,0:T(8,128)(2,1)} %all-gather.2.cloned.1.call-done), kind=kOutput, calls=%fused_computation.32 | convolution fusion | flops 537001984 | bytes 4980736 | tf_op jit(solution)/shard_map/dot_general | solution.py:88
  (5 shorter events, 0.0 us)
Async XLA Ops:
  6.5 23.0 %copy-start.2 = (bf16[128,1024]{1,0:T(8,128)(2,1)S(1)}, bf16[128,1024]{1,0:T(8,128)(2,1)}, u32[]{:S(2)}) copy-start(bf16[128,1024]{1,0:T(8,128)(2,1)} %param.9) | copy-start | bytes 786436
  6.5 24.0 %copy-start.1 = (bf16[2,2,128,1024]{3,2,1,0:T(8,128)(2,1)S(1)}, bf16[2,2,128,1024]{3,2,1,0:T(8,128)(2,1)}, u32[]{:S(2)}) copy-start(bf16[2,2,128,1024]{3,2,1,0:T(8,128)(2,1)} %param.12) | copy-start | bytes 3145732
  8.6 26.7 %copy-start.3 = (bf16[128,1024]{1,0:T(8,128)(2,1)S(1)}, bf16[128,1024]{1,0:T(8,128)(2,1)}, u32[]{:S(2)}) copy-start(bf16[128,1024]{1,0:T(8,128)(2,1)} %param.10) | copy-start | bytes 786436
  8.6 16.3 %all-to-all-start.4 = ((bf16[128,8,128]{2,0,1:T(8,128)(2,1)}), bf16[128,8,128]{2,0,1:T(8,128)(2,1)S(1)}, u32[]{:S(2)}, u32[]{:S(2)}) async-start(bf16[128,8,128]{2,0,1:T(8,128)(2,1)} %copy.81), calls=%async_computation.4 | async-start | bytes 524288 | tf_op jit(solution)/shard_map/all_to_all | solution.py:70
  24.9 43.9 %all-to-all-start.3 = ((bf16[2,2,128,1024]{2,1,0,3:T(2,128)(2,1)}), bf16[2,2,128,1024]{2,1,0,3:T(2,128)(2,1)S(1)}, u32[]{:S(2)}, u32[]{:S(2)}) async-start(bf16[2,2,128,1024]{2,1,0,3:T(2,128)(2,1)} %copy.78), calls=%async_computation.3 | async-start | bytes 2097152 | tf_op jit(solution)/shard_map/all_to_all | solution.py:75
  28.5 150.6 %all-gather.2.cloned.1.call-start = ((), (), s32[]{:S(2)}) async-start(), calls=%async_computation.6 | async-start | bytes 4718592 | tf_op jit(solution)/shard_map/all_gather | solution.py:90
  68.8 54.1 %all-to-all-start.1 = ((bf16[2,2,128,1024]{2,1,0,3:T(2,128)(2,1)}), bf16[2,2,128,1024]{2,1,0,3:T(2,128)(2,1)}, u32[]{:S(2)}, u32[]{:S(2)}) async-start(bf16[2,2,128,1024]{2,1,0,3:T(2,128)(2,1)} %copy.73), calls=%async_computation.1 | async-start | bytes 2097152 | tf_op jit(solution)/shard_map/all_to_all | solution.py:76
  75.4 2.5 %copy-start = (f32[16,128,128]{2,0,1:T(8,128)S(1)}, f32[16,128,128]{2,0,1:T(8,128)}, u32[]{:S(2)}) copy-start(f32[16,128,128]{2,0,1:T(8,128)} %get-tuple-element.10) | copy-start | bytes 3145732
  122.9 14.7 %all-to-all-start.2 = ((bf16[128,8,128]{2,0,1:T(8,128)(2,1)}), bf16[128,8,128]{2,0,1:T(8,128)(2,1)}, u32[]{:S(2)}, u32[]{:S(2)}) async-start(bf16[128,8,128]{2,0,1:T(8,128)(2,1)} %copy.76), calls=%async_computation.2 | async-start | bytes 524288 | tf_op jit(solution)/shard_map/all_to_all | solution.py:71
  137.7 24.2 %all-to-all-start = ((bf16[128,8,128]{2,0,1:T(8,128)(2,1)}), bf16[128,8,128]{2,0,1:T(8,128)(2,1)S(1)}, u32[]{:S(2)}, u32[]{:S(2)}) async-start(bf16[128,8,128]{2,0,1:T(8,128)(2,1)} %copy.71), calls=%async_computation | async-start | bytes 524288 | tf_op jit(solution)/shard_map/all_to_all | solution.py:72
  158.0 3.8 %copy-start.4 = (f32[128]{0:T(128)S(1)}, f32[128]{0:T(128)}, u32[]{:S(2)}) copy-start(f32[128]{0:T(128)} %dynamic_slice.7) | copy-start | bytes 1540
Sparse Core Ops, SparseCore 0:
  31.5 104.5 all-gather.1
where the time goes:
time: 191 us; the launch traced here: 190 us
  waiting for transfers between devices  75.3 us (39%)
  matrix products  37.8 us (20%)
  starting transfers between devices  25.4 us (13%)
  local copies, waits for them, and re-layouts  21.1 us (11%)
  blocking collectives  16.2 us (8%)
  between operations  13.7 us (7%)
    all_to_all x1, waiting for transfers between devices, shards(): lax.all_to_all(spectrum_second, 'seq', split_axis=3, concat_axis=1, tiled...  40.1 us
    dot_general x20, matrix products, mixing(): return jnp.einsum(form, left, right, precision=lax.Precision.HIGHEST)  34.2 us
    all_to_all x1, waiting for transfers between devices, shards(): lax.all_to_all(spectrum_first, 'seq', split_axis=3, concat_axis=1, tiled=...  29.2 us
    all_to_all x1, blocking collectives, shards(): lax.all_to_all(mixed_cols, 'seq', split_axis=0, concat_axis=1, tiled=True)  14 us
    all_to_all x1, starting transfers between devices, shards(): lax.all_to_all(signal, 'seq', split_axis=1, concat_axis=0, tiled=True)  7.38 us
    unnamed x15, local copies, waits for them, and re-layouts  7.3 us
    all_to_all x1, starting transfers between devices, shards(): lax.all_to_all(gate_second, 'seq', split_axis=1, concat_axis=0, tiled=True)  5.69 us
    all_to_all x1, waiting for transfers between devices, shards(): lax.all_to_all(signal, 'seq', split_axis=1, concat_axis=0, tiled=True)  5.23 us
  transfers between devices with their start and end apart: 6, of which 3 were waited for; matrix products, arithmetic and copies ran while one was open for 28% of the time, Pallas kernels for 0%

commit v1 on v0

--- a/solution.py
+++ b/solution.py
@@ -3,6 +3,29 @@
 import jax.numpy as jnp
 from jax import lax
 from jax.sharding import PartitionSpec as P
+
+
+def split_up(x, dim, length):
+    shape = x.shape
+    pieces = x.reshape(*shape[:dim], length, shape[dim] // length, *shape[dim + 1 :])
+    return jnp.moveaxis(pieces, dim, 0)
+
+
+def in_order(blocks, dim):
+    blocks = jnp.moveaxis(blocks, 0, dim)
+    dims = blocks.shape
+    return blocks.reshape(*dims[:dim], dims[dim] * dims[dim + 1], *dims[dim + 2 :])
+
+
+def swapped_with_each(x, axis, split_dim, concat_dim):
+    peers, position = (lax.axis_size(axis), lax.axis_index(axis))
+    blocks = split_up(x, split_dim, peers)
+    finished = [blocks[position]]
+    for turn in range(1, peers):
+        sent = blocks[position ^ turn]
+        finished.append(lax.ppermute(sent, axis, [(i, i ^ turn) for i in range(peers)]))
+    blocks = jnp.stack(finished)[position ^ jnp.arange(peers)]
+    return in_order(blocks, concat_dim)
 
 
 def angle_grid(first, second, modulus):
@@ -73,7 +96,7 @@
     )
     spec_one, spec_two = (
         lax.all_to_all(spectrum_first, "seq", split_axis=3, concat_axis=1, tiled=True),
-        lax.all_to_all(spectrum_second, "seq", split_axis=3, concat_axis=1, tiled=True),
+        swapped_with_each(spectrum_second, "seq", 3, 1),
     )
     skip_one = lax.dynamic_slice_in_dim(skip_first, seq_index * cols, cols, 0)
     skip_two = lax.dynamic_slice_in_dim(skip_second, seq_index * cols, cols, 0)

time: 191 us -> 167 us (0.87)
  waiting for transfers between devices: 75.3 us -> 31.1 us
  starting transfers between devices: 25.4 us -> 34.5 us
  local copies, waits for them, and re-layouts: 21.1 us -> 28.8 us
  other arithmetic: 0.06 us -> 2.58 us
    all_to_all x1 -> x0, waiting for transfers between devices: 40.1 us -> none  [shards(): lax.all_to_all(spectrum_second, 'seq', split_axis=3, concat_axis=1, tiled...]
    ppermute x0 -> x7, starting transfers between devices: none -> 11.3 us  [swapped_with_each(): lax.ppermute(sent, axis, [(i, i ^ turn) for i in range(peers)])]
    all_to_all x1, waiting for transfers between devices: 5.23 us -> 0.01 us  [shards(): lax.all_to_all(signal, 'seq', split_axis=1, concat_axis=0, tiled=True)]
    all_to_all x1 -> x0, starting transfers between devices: 4.43 us -> none  [shards(): lax.all_to_all(spectrum_second, 'seq', split_axis=3, concat_axis=1, tiled...]
    another operation x0 -> x10, local copies, waits for them, and re-layouts: none -> 3.8 us
    ppermute x0 -> x7, waiting for transfers between devices: none -> 3.09 us  [swapped_with_each(): lax.ppermute(sent, axis, [(i, i ^ turn) for i in range(peers)])]
    unnamed x15 -> x24, local copies, waits for them, and re-layouts: 7.3 us -> 10.1 us
    all_to_all x1, starting transfers between devices: 3.59 us -> 5.94 us  [shards(): lax.all_to_all(spectrum_first, 'seq', split_axis=3, concat_axis=1, tiled=...]
  transfers between devices with their start and end apart: 6 -> 12, of which waited for: 3 -> 3; matrix products, arithmetic and copies ran while one was open for 28% -> 39% of each run, Pallas kernels for 0% -> 0%
where the time goes in v1:
time: 167 us; the launch traced here: 166 us
  matrix products  38.6 us (23%)
  starting transfers between devices  34.5 us (21%)
  waiting for transfers between devices  31.1 us (19%)
  local copies, waits for them, and re-layouts  28.8 us (17%)
  blocking collectives  16.2 us (10%)
  between operations  13.9 us (8%)
  other arithmetic  2.58 us (2%)
    dot_general x20, matrix products, mixing(): return jnp.einsum(form, left, right, precision=lax.Precision.HIGHEST)  34.9 us
    all_to_all x1, waiting for transfers between devices, shards(): lax.all_to_all(spectrum_first, 'seq', split_axis=3, concat_axis=1, tiled=...  27 us
    all_to_all x1, blocking collectives, shards(): lax.all_to_all(mixed_cols, 'seq', split_axis=0, concat_axis=1, tiled=True)  14 us
    ppermute x7, starting transfers between devices, swapped_with_each(): lax.ppermute(sent, axis, [(i, i ^ turn) for i in range(peers)])  11.3 us
    unnamed x24, local copies, waits for them, and re-layouts  10.1 us
    all_to_all x1, starting transfers between devices, shards(): lax.all_to_all(signal, 'seq', split_axis=1, concat_axis=0, tiled=True)  7.25 us
    all_to_all x1, starting transfers between devices, shards(): lax.all_to_all(spectrum_first, 'seq', split_axis=3, concat_axis=1, tiled=...  5.94 us
    all_to_all x1, starting transfers between devices, shards(): lax.all_to_all(gate_second, 'seq', split_axis=1, concat_axis=0, tiled=True)  5.03 us
  transfers between devices with their start and end apart: 12, of which 3 were waited for; matrix products, arithmetic and copies ran while one was open for 39% of the time, Pallas kernels for 0%

profile of v1, /device:TPU:0, one launch (start us, length us, event | category | flops | bytes accessed | tf_op | source)
XLA Modules:
  0.0 165.7 jit_solution(2838424728027881409)
XLA Ops:
  6.5 1.2 copy.144
  7.7 0.9 copy.145
  8.6 7.3 %all-to-all-start.3 = ((bf16[128,8,128]{2,0,1:T(8,128)(2,1)}), bf16[128,8,128]{2,0,1:T(8,128)(2,1)S(1)}, u32[]{:S(2)}, u32[]{:S(2)}) async-start(bf16[128,8,128]{2,0,1:T(8,128)(2,1)} %copy.145), calls=%async_computation.3 | async-start | bytes 524288 | tf_op jit(solution)/shard_map/all_to_all | solution.py:93
  15.9 1.6 copy.129
  17.6 0.8 constant_dynamic-slice_fusion
  18.4 0.8 copy.131
  19.2 1.9 %collective-permute-start = (bf16[2,2,128,128]{3,2,1,0:T(8,128)(2,1)}, bf16[2,2,128,128]{3,2,1,0:T(8,128)(2,1)}, u32[]{:S(2)}, u32[]{:S(2)}) collective-permute-start(bf16[2,2,128,128]{3,2,1,0:T(8,128)(2,1)} %bitcast.5), channel_id=1, source_target_pairs={{0,2},{2,0},{4,6},{6,4},{8,10},{10,8},{12,14},{14,12},{1,3},{3,1},... | collective-permute-start | bytes 393224 | tf_op jit(solution)/shard_map/ppermute | solution.py:26
  21.1 0.8 copy.132
  21.9 1.5 collective-permute-start.1
  23.4 0.8 copy.133
  24.4 2.9 %collective-permute-start.3 = (bf16[2,2,128,128]{3,2,1,0:T(8,128)(2,1)S(1)}, bf16[2,2,128,128]{3,2,1,0:T(8,128)(2,1)S(1)}, u32[]{:S(2)}, u32[]{:S(2)}) collective-permute-start(bf16[2,2,128,128]{3,2,1,0:T(8,128)(2,1)S(1)} %bitcast.166), channel_id=1, source_target_pairs={{0,8},{2,10},{4,12},{6,14},{8,0},{10,2},{12,4},{14,6},{1,9},{3,11}... | collective-permute-start | bytes 393224 | tf_op jit(solution)/shard_map/ppermute | solution.py:26
  27.4 1.5 collective-permute-start.4
  29.2 0.6 fusion.118
  30.0 2.1 %copy.142 = bf16[2,2,128,1024]{2,1,0,3:T(2,128)(2,1)} copy(bf16[2,2,128,1024]{3,2,1,0:T(8,128)(2,1)S(1)} %copy-done.2) | data formatting | bytes 2097152 | tf_op args[3]
  32.0 1.1 copy.139
  33.1 0.8 copy.140
  34.3 1.3 dynamic_slice.7
  35.5 1.3 dynamic_slice.8
  36.9 1.1 copy.126
  38.0 0.9 copy.127
  38.9 0.7 pad_clamp_fusion
  39.6 3.3 %collective-permute-start.5 = (bf16[2,2,128,128]{3,2,1,0:T(8,128)(2,1)S(1)}, bf16[2,2,128,128]{3,2,1,0:T(8,128)(2,1)S(1)}, u32[]{:S(2)}, u32[]{:S(2)}) collective-permute-start(bf16[2,2,128,128]{3,2,1,0:T(8,128)(2,1)S(1)} %bitcast.168), channel_id=1, source_target_pairs={{0,12},{2,14},{4,8},{6,10},{8,4},{10,6},{12,0},{14,2},{1,13},{3,15... | collective-permute-start | bytes 393224 | tf_op jit(solution)/shard_map/ppermute | solution.py:26
  42.8 0.9 bitcast_dynamic-update-slice_fusion.6
  43.9 0.9 bitcast_dynamic-update-slice_fusion.5
  44.8 0.9 bitcast_dynamic-update-slice_fusion.4
  45.9 5.9 %all-to-all-start.2 = ((bf16[2,2,128,1024]{2,1,0,3:T(2,128)(2,1)}), bf16[2,2,128,1024]{2,1,0,3:T(2,128)(2,1)}, u32[]{:S(2)}, u32[]{:S(2)}) async-start(bf16[2,2,128,1024]{2,1,0,3:T(2,128)(2,1)} %copy.142), calls=%async_computation.2 | async-start | bytes 2097152 | tf_op jit(solution)/shard_map/all_to_all | solution.py:98
  51.8 3.1 %collective-permute-done.6 = bf16[2,2,128,128]{3,2,1,0:T(8,128)(2,1)S(1)} collective-permute-done((bf16[2,2,128,128]{3,2,1,0:T(8,128)(2,1)S(1)}, bf16[2,2,128,128]{3,2,1,0:T(8,128)(2,1)S(1)}, u32[]{:S(2)}, u32[]{:S(2)}) %collective-permute-start.6) | collective-permute-done | bytes 131104 | tf_op jit(solution)/shard_map/ppermute | solution.py:26
  54.9 0.7 gather_fusion
  55.7 1.2 slice_convert_fusion.1
  56.9 0.3 copy.138
  57.3 1.6 copy.156
  58.8 0.7 convolution_negate_fusion.1
  59.5 2.6 %fusion.180 = (f32[16,128,128]{2,0,1:T(8,128)S(1)}, f32[16,128,128]{2,0,1:T(8,128)S(1)}, f32[16,128,128]{2,0,1:T(8,128)}) fusion(f32[16,128]{0,1:T(8,128)S(1)} %copy.148, f32[16,128,128]{2,0,1:T(8,128)S(1)} %convolution_negate_fusion.1, f32[16,128]{0,1:T(8,128)S(1)} %copy.147, bf16[128,8,128]{2,0,1:T(8,128)(2,1)S(1)} %all-to-all-done.3), kind=kOutput, calls=%fused_computation.226 | convolution fusion | flops 27002624 | bytes 4472832 | tf_op jit(solution)/shard_map/ka,amc->kmc/dot_general | solution.py:38
  62.1 2.1 %fusion.22 = f32[16,128,128]{2,1,0:T(8,128)S(1)} fusion(f32[16,128,128]{2,0,1:T(8,128)S(1)} %get-tuple-element.8), kind=kOutput, calls=%fused_computation.44 | convolution fusion | flops 402882560 | bytes 2097152 | tf_op jit(solution)/shard_map/qm,kmc->kqc/dot_general | solution.py:38
  64.2 3.2 %fusion.3 = f32[16,128,128]{1,2,0:T(8,128)} fusion(f32[16,128,128]{2,1,0:T(8,128)S(1)} %fusion.22, f32[16,128,128]{2,0,1:T(8,128)S(1)} %get-tuple-element.9), kind=kOutput, calls=%fused_computation.13 | convolution fusion | flops 403177472 | bytes 3145728 | tf_op jit(solution)/shard_map/qm,kmc->kqc/dot_general | solution.py:38
  67.4 27.0 %all-to-all-done.2 = bf16[2,2,128,1024]{2,1,0,3:T(2,128)(2,1)} async-done(((bf16[2,2,128,1024]{2,1,0,3:T(2,128)(2,1)}), bf16[2,2,128,1024]{2,1,0,3:T(2,128)(2,1)}, u32[]{:S(2)}, u32[]{:S(2)}) %all-to-all-start.2) | async-done | bytes 1048608 | tf_op jit(solution)/shard_map/all_to_all | solution.py:98
  94.5 4.9 %all-to-all-start.1 = ((bf16[128,8,128]{2,0,1:T(8,128)(2,1)}), bf16[128,8,128]{2,0,1:T(8,128)(2,1)}, u32[]{:S(2)}, u32[]{:S(2)}) async-start(bf16[128,8,128]{2,0,1:T(8,128)(2,1)} %copy.140), calls=%async_computation.1 | async-start | bytes 524288 | tf_op jit(solution)/shard_map/all_to_all | solution.py:94
  99.4 1.6 copy.192
  101.2 2.4 %fusion.13 = (f32[16,128,128]{1,2,0:T(8,128)S(1)}, f32[16,128,128]{1,2,0:T(8,128)S(1)}) fusion(f32[16,128,128]{1,2,0:T(8,128)S(1)} %copy-done, bf16[1,8,2,128,128]{3,4,2,1,0:T(8,128)(2,1)S(1)} %get-tuple-element.30, bf16[1,8,2,128,128]{3,4,2,1,0:T(8,128)(2,1)S(1)} %get-tuple-element.29, f32[16,128,128]{2,1,0:T(8,128)S(1)} %fusion.22, ...), kind=kOutput, calls=%fused_computation.31 | convolution fusion | flops 405274624 | bytes 6291456 | tf_op jit(solution)/shard_map/qm,kmc->kqc/dot_general | solution.py:38
  103.6 1.2 fusion.26
  104.8 1.3 convolution_add_fusion.2
  106.1 2.4 %add_bitcast_fusion.1 = (f32[16,128,128]{1,2,0:T(8,128)S(1)}, f32[16,128,128]{1,2,0:T(8,128)}) fusion(f32[16,128,128]{2,1,0:T(8,128)S(1)} %convolution_add_fusion.2, f32[16,128]{1,0:T(8,128)S(1)} %get-tuple-element.31, f32[16,128]{1,0:T(8,128)S(1)} %get-tuple-element.32, f32[16,128,128]{2,1,0:T(8,128)S(1)} %fusion.26, f32[16,128,128]{1,2,0:T(8,128)S(1)} %get-tuple-element.13), kind=kOutput, calls=%fused_computation.53 | convolution fusion | flops 404733952 | bytes 5259264 | tf_op jit(solution)/shard_map/mq,kqc->kmc/dot_general | solution.py:38
  108.5 2.6 %copy.152 = f32[16,128,128]{2,0,1:T(8,128)} copy(f32[16,128,128]{1,2,0:T(8,128)} %get-tuple-element.18) | data formatting | bytes 2097152 | tf_op jit(solution)/shard_map/sub | solution.py:72
  111.1 1.4 copy.153
  112.5 1.9 %fusion.80 = f32[8,128,128]{2,0,1:T(8,128)S(1)} fusion(f32[16,128,128]{2,0,1:T(8,128)} %copy.152), kind=kOutput, calls=%fused_computation.125 | convolution fusion | flops 25167616 | bytes 1572864 | tf_op jit(solution)/shard_map/ka,kmc->amc/dot_general | solution.py:38
  114.4 1.0 all-to-all-done.1
  115.4 5.0 %all-to-all-start = ((bf16[128,8,128]{2,0,1:T(8,128)(2,1)}), bf16[128,8,128]{2,0,1:T(8,128)(2,1)}, u32[]{:S(2)}, u32[]{:S(2)}) async-start(bf16[128,8,128]{2,0,1:T(8,128)(2,1)} %copy.127), calls=%async_computation | async-start | bytes 524288 | tf_op jit(solution)/shard_map/all_to_all | solution.py:95
  120.4 2.2 %fusion.11 = bf16[8,128,128]{2,0,1:T(8,128)(2,1)S(1)} fusion(f32[8,128,128]{2,0,1:T(8,128)S(1)} %fusion.80, f32[16,128,128]{2,0,1:T(8,128)} %copy.153, bf16[128,8,128]{2,0,1:T(8,128)(2,1)} %all-to-all-done.1, f32[128]{0:T(128)} %dynamic_slice.7, bf16[128,8,128]{2,0,1:T(8,128)(2,1)S(1)} %all-to-all-done.3), kind=kOutput, calls=%fused_computation.28 | convolution fusion | flops 26216192 | bytes 2359808 | tf_op jit(solution)/shard_map/ka,kmc->amc/dot_general | solution.py:38
  122.7 0.7 convolution_negate_fusion
  123.4 1.1 fusion.179
  124.4 2.1 %fusion.18 = f32[16,128,128]{2,1,0:T(8,128)S(1)} fusion(f32[16,128,128]{2,0,1:T(8,128)S(1)} %get-tuple-element.5), kind=kOutput, calls=%fused_computation.40 | convolution fusion | flops 402882560 | bytes 2097152 | tf_op jit(solution)/shard_map/qm,kmc->kqc/dot_general | solution.py:38
  126.6 2.2 %fusion = f32[16,128,128]{1,2,0:T(8,128)S(1)} fusion(f32[16,128,128]{2,1,0:T(8,128)S(1)} %fusion.18, f32[16,128,128]{2,0,1:T(8,128)S(1)} %get-tuple-element.7), kind=kOutput, calls=%fused_computation.4 | convolution fusion | flops 403177472 | bytes 3145728 | tf_op jit(solution)/shard_map/qm,kmc->kqc/dot_general | solution.py:38
  128.8 2.3 %fusion.15 = (f32[16,128,128]{1,2,0:T(8,128)S(1)}, f32[16,128,128]{1,2,0:T(8,128)S(1)}) fusion(f32[1,8,2,128,128]{3,4,2,1,0:T(8,128)S(1)} %copy.156, f32[16,128,128]{1,2,0:T(8,128)S(1)} %fusion, f32[1,8,2,128,128]{3,4,2,1,0:T(8,128)S(1)} %copy.138, f32[16,128,128]{2,1,0:T(8,128)S(1)} %fusion.18, f32[16,128,128]{2,0,1:T(8,128)S(1)} %get-tuple-element.6), kind=kOutput, calls=%fused_computation.35 | convolution fusion | flops 404750336 | bytes 7340032 | tf_op jit(solution)/shard_map/qm,kmc->kqc/dot_general | solution.py:38
  131.1 1.2 fusion.24
  132.3 1.3 convolution_add_fusion
  133.6 1.7 %add_bitcast_fusion = (f32[16,128,128]{1,2,0:T(8,128)S(1)}, f32[16,128,128]{1,2,0:T(8,128)S(1)}) fusion(f32[16,128,128]{2,1,0:T(8,128)S(1)} %convolution_add_fusion, f32[16,128]{1,0:T(8,128)S(1)} %get-tuple-element.31, f32[16,128]{1,0:T(8,128)S(1)} %get-tuple-element.32, f32[16,128,128]{2,1,0:T(8,128)S(1)} %fusion.24, f32[16,128,128]{1,2,0:T(8,128)S(1)} %get-tuple-element.11), kind=kOutput, calls=%fused_computation.47 | convolution fusion | flops 404733952 | bytes 5259264 | tf_op jit(solution)/shard_map/mq,kqc->kmc/dot_general | solution.py:38
  135.3 0.5 copy.158
  135.8 0.5 copy.159
  136.3 0.6 fusion.76
  137.0 1.7 %fusion.10 = bf16[8,128,128]{2,0,1:T(8,128)(2,1)S(1)} fusion(f32[8,128,128]{2,0,1:T(8,128)S(1)} %fusion.76, f32[16,128,128]{2,0,1:T(8,128)S(1)} %copy.159, bf16[8,128,128]{2,0,1:T(8,128)(2,1)S(1)} %fusion.11, bf16[128,8,128]{2,0,1:T(8,128)(2,1)} %all-to-all-done, f32[128]{0:T(128)S(1)} %copy-done.5), kind=kOutput, calls=%fused_computation.27 | convolution fusion | flops 26216192 | bytes 2359808 | tf_op jit(solution)/shard_map/ka,kmc->amc/dot_general | solution.py:38
  138.8 14.0 %all_to_all.73 = bf16[8,128,128]{2,1,0:T(8,128)(2,1)S(1)} all-to-all(bf16[8,128,128]{2,1,0:T(8,128)(2,1)S(1)} %copy.160), channel_id=1, replica_groups=mesh['grp'=2,'seq'=8,'mdl'=2] {'seq'}, dimensions={0} | all-to-all | bytes 524288 | tf_op jit(solution)/shard_map/all_to_all | solution.py:109
  152.8 0.2 copy.161
  153.0 2.2 %all_gather.6 = bf16[128,2048]{0,1:T(8,128)(2,1)S(1)} all-gather(bf16[128,1024]{0,1:T(8,128)(2,1)S(1)} %bitcast.161), channel_id=1, replica_groups=mesh['grp'=2,'seq'=8,'mdl'=2] {'mdl'}, dimensions={1}, use_global_device_ids=true | all-gather | bytes 786432 | tf_op jit(solution)/shard_map/all_gather | solution.py:110
  155.2 3.6 %convolution_convert_fusion = bf16[128,1024]{1,0:T(8,128)(2,1)} fusion(bf16[128,2048]{0,1:T(8,128)(2,1)S(1)} %all_gather.6, bf16[2048,1024]{1,0:T(8,128)(2,1)} %all-gather.2.cloned.1.call-done), kind=kOutput, calls=%fused_computation.29 | convolution fusion | flops 537001984 | bytes 4980736 | tf_op jit(solution)/shard_map/dot_general | solution.py:111
  (40 shorter events, 1.6 us)
Async XLA Ops:
  6.5 23.4 %copy-start.2 = (bf16[2,2,128,1024]{3,2,1,0:T(8,128)(2,1)S(1)}, bf16[2,2,128,1024]{3,2,1,0:T(8,128)(2,1)}, u32[]{:S(2)}) copy-start(bf16[2,2,128,1024]{3,2,1,0:T(8,128)(2,1)} %param.11) | copy-start | bytes 3145732
  8.6 37.2 %all-to-all-start.3 = ((bf16[128,8,128]{2,0,1:T(8,128)(2,1)}), bf16[128,8,128]{2,0,1:T(8,128)(2,1)S(1)}, u32[]{:S(2)}, u32[]{:S(2)}) async-start(bf16[128,8,128]{2,0,1:T(8,128)(2,1)} %copy.145), calls=%async_computation.3 | async-start | bytes 524288 | tf_op jit(solution)/shard_map/all_to_all | solution.py:93
  15.9 139.3 %all-gather.2.cloned.1.call-start = ((), (), s32[]{:S(2)}) async-start(), calls=%async_computation.5 | async-start | bytes 4718592 | tf_op jit(solution)/shard_map/all_gather | solution.py:113
  18.4 15.6 %copy-start.4 = (bf16[2,2,128,1,128]{2,4,3,1,0:T(8,128)(2,1)S(1)}, bf16[2,2,128,1,128]{2,4,3,1,0:T(8,128)(2,1)}, u32[]{:S(2)}) copy-start(bf16[2,2,128,1,128]{2,4,3,1,0:T(8,128)(2,1)} %get-tuple-element.22) | copy-start | bytes 393220
  18.4 15.7 %copy-start.3 = (bf16[2,2,128,1,128]{2,4,3,1,0:T(8,128)(2,1)S(1)}, bf16[2,2,128,1,128]{2,4,3,1,0:T(8,128)(2,1)}, u32[]{:S(2)}) copy-start(bf16[2,2,128,1,128]{2,4,3,1,0:T(8,128)(2,1)} %get-tuple-element.21) | copy-start | bytes 393220
  19.2 20.4 %collective-permute-start = (bf16[2,2,128,128]{3,2,1,0:T(8,128)(2,1)}, bf16[2,2,128,128]{3,2,1,0:T(8,128)(2,1)}, u32[]{:S(2)}, u32[]{:S(2)}) collective-permute-start(bf16[2,2,128,128]{3,2,1,0:T(8,128)(2,1)} %bitcast.5), channel_id=1, source_target_pairs={{0,2},{2,0},{4,6},{6,4},{8,10},{10,8},{12,14},{14,12},{1,3},{3,1},... | collective-permute-start | bytes 393224 | tf_op jit(solution)/shard_map/ppermute | solution.py:26
  21.9 21.9 %collective-permute-start.1 = (bf16[2,2,128,128]{3,2,1,0:T(8,128)(2,1)}, bf16[2,2,128,128]{3,2,1,0:T(8,128)(2,1)}, u32[]{:S(2)}, u32[]{:S(2)}) collective-permute-start(bf16[2,2,128,128]{3,2,1,0:T(8,128)(2,1)} %bitcast.7), channel_id=1, source_target_pairs={{0,4},{2,6},{4,0},{6,2},{8,12},{10,14},{12,8},{14,10},{1,5},{3,7},... | collective-permute-start | bytes 393224 | tf_op jit(solution)/shard_map/ppermute | solution.py:26
  24.1 20.7 %collective-permute-start.2 = (bf16[2,2,128,128]{3,2,1,0:T(8,128)(2,1)}, bf16[2,2,128,128]{3,2,1,0:T(8,128)(2,1)}, u32[]{:S(2)}, u32[]{:S(2)}) collective-permute-start(bf16[2,2,128,128]{3,2,1,0:T(8,128)(2,1)} %bitcast.9), channel_id=1, source_target_pairs={{0,6},{2,4},{4,2},{6,0},{8,14},{10,12},{12,10},{14,8},{1,7},{3,5},... | collective-permute-start | bytes 393224 | tf_op jit(solution)/shard_map/ppermute | solution.py:26
  24.4 21.4 %collective-permute-start.3 = (bf16[2,2,128,128]{3,2,1,0:T(8,128)(2,1)S(1)}, bf16[2,2,128,128]{3,2,1,0:T(8,128)(2,1)S(1)}, u32[]{:S(2)}, u32[]{:S(2)}) collective-permute-start(bf16[2,2,128,128]{3,2,1,0:T(8,128)(2,1)S(1)} %bitcast.166), channel_id=1, source_target_pairs={{0,8},{2,10},{4,12},{6,14},{8,0},{10,2},{12,4},{14,6},{1,9},{3,11}... | collective-permute-start | bytes 393224 | tf_op jit(solution)/shard_map/ppermute | solution.py:26
  27.4 18.4 %collective-permute-start.4 = (bf16[2,2,128,128]{3,2,1,0:T(8,128)(2,1)S(1)}, bf16[2,2,128,128]{3,2,1,0:T(8,128)(2,1)S(1)}, u32[]{:S(2)}, u32[]{:S(2)}) collective-permute-start(bf16[2,2,128,128]{3,2,1,0:T(8,128)(2,1)S(1)} %bitcast.165), channel_id=1, source_target_pairs={{0,10},{2,8},{4,14},{6,12},{8,2},{10,0},{12,6},{14,4},{1,11},{3,9}... | collective-permute-start | bytes 393224 | tf_op jit(solution)/shard_map/ppermute | solution.py:26
  39.6 12.2 %collective-permute-start.5 = (bf16[2,2,128,128]{3,2,1,0:T(8,128)(2,1)S(1)}, bf16[2,2,128,128]{3,2,1,0:T(8,128)(2,1)S(1)}, u32[]{:S(2)}, u32[]{:S(2)}) collective-permute-start(bf16[2,2,128,128]{3,2,1,0:T(8,128)(2,1)S(1)} %bitcast.168), channel_id=1, source_target_pairs={{0,12},{2,14},{4,8},{6,10},{8,4},{10,6},{12,0},{14,2},{1,13},{3,15... | collective-permute-start | bytes 393224 | tf_op jit(solution)/shard_map/ppermute | solution.py:26
  43.8 11.1 %collective-permute-start.6 = (bf16[2,2,128,128]{3,2,1,0:T(8,128)(2,1)S(1)}, bf16[2,2,128,128]{3,2,1,0:T(8,128)(2,1)S(1)}, u32[]{:S(2)}, u32[]{:S(2)}) collective-permute-start(bf16[2,2,128,128]{3,2,1,0:T(8,128)(2,1)S(1)} %bitcast.167), channel_id=1, source_target_pairs={{0,14},{2,12},{4,10},{6,8},{8,6},{10,4},{12,2},{14,0},{1,15},{3,13... | collective-permute-start | bytes 393224 | tf_op jit(solution)/shard_map/ppermute | solution.py:26
  45.9 48.6 %all-to-all-start.2 = ((bf16[2,2,128,1024]{2,1,0,3:T(2,128)(2,1)}), bf16[2,2,128,1024]{2,1,0,3:T(2,128)(2,1)}, u32[]{:S(2)}, u32[]{:S(2)}) async-start(bf16[2,2,128,1024]{2,1,0,3:T(2,128)(2,1)} %copy.142), calls=%async_computation.2 | async-start | bytes 2097152 | tf_op jit(solution)/shard_map/all_to_all | solution.py:98
  94.5 20.9 %all-to-all-start.1 = ((bf16[128,8,128]{2,0,1:T(8,128)(2,1)}), bf16[128,8,128]{2,0,1:T(8,128)(2,1)}, u32[]{:S(2)}, u32[]{:S(2)}) async-start(bf16[128,8,128]{2,0,1:T(8,128)(2,1)} %copy.140), calls=%async_computation.1 | async-start | bytes 524288 | tf_op jit(solution)/shard_map/all_to_all | solution.py:94
  99.4 1.7 %copy-start = (f32[16,128,128]{1,2,0:T(8,128)S(1)}, f32[16,128,128]{1,2,0:T(8,128)}, u32[]{:S(2)}) copy-start(f32[16,128,128]{1,2,0:T(8,128)} %fusion.3) | copy-start | bytes 3145732
  99.4 1.9 %copy-start.1 = (f32[16,128,128]{2,0,1:T(8,128)S(1)}, f32[16,128,128]{2,0,1:T(8,128)}, u32[]{:S(2)}) copy-start(f32[16,128,128]{2,0,1:T(8,128)} %get-tuple-element.10) | copy-start | bytes 3145732
  115.4 21.6 %all-to-all-start = ((bf16[128,8,128]{2,0,1:T(8,128)(2,1)}), bf16[128,8,128]{2,0,1:T(8,128)(2,1)}, u32[]{:S(2)}, u32[]{:S(2)}) async-start(bf16[128,8,128]{2,0,1:T(8,128)(2,1)} %copy.127), calls=%async_computation | async-start | bytes 524288 | tf_op jit(solution)/shard_map/all_to_all | solution.py:95
  135.3 1.7 %copy-start.5 = (f32[128]{0:T(128)S(1)}, f32[128]{0:T(128)}, u32[]{:S(2)}) copy-start(f32[128]{0:T(128)} %dynamic_slice.8) | copy-start | bytes 1540
Sparse Core Ops, SparseCore 0:
  29.1 107.9 all-gather.1
